TPU v7x, 32 devices: a whole 2x2x4 slice. The times are simulated.
32 devices in a mesh: sector: 4 (over x, core), op: 8 (over z, y).
Axes of the slice: x: 2, y: 2, z: 4, core: 2. Of those that a mesh axis runs over, the one named last changes fastest.
Arguments:
- wave: float32 [8, 768, 768], P('sector', 'op'), may hold values from -6 to 6
- onsite: float32 [8, 768, 768], P('sector', 'op'), may hold values from -2 to 2
- left_ops: float32 [8, 16, 768, 768], P('sector', 'op'), may hold values from -0.21875 to 0.21875
- right_ops: float32 [8, 16, 768, 768], P('sector', 'op'), may hold values from -0.0546875 to 0.0546875
- coupling: int32 [8, 16], P('sector', 'op'), may hold values from 0 to 2
Outputs:
- sigma: float32 [8, 768, 768], P('sector', 'op')
- correction: float32 [8, 768, 768], P('sector', 'op')
All inputs are finite; a program needn't handle non-finite values.
Results may differ from a plain program's by a relative error of at most 0.0001.
Values sent between devices are 32-bit elements; how exact they have to be, the bound alone decides.
No kernel may reach another device: no remote copies, remote signals or barrier semaphores. Data moves between devices by JAX's collectives and lax.ppermute only.
A program may use at most 128 MiB of HBM per device.

v0:
```python
import jax
import jax.numpy as jnp
from jax import lax
from jax.sharding import PartitionSpec as P


def shifted(value, axis, by):
    length = lax.axis_size(axis)
    return lax.ppermute(value, axis, [(i, (i + by) % length) for i in range(length)])


def on_device(wave, onsite, left_ops, right_ops, coupling):
    highest = lax.Precision.HIGHEST
    rows = wave.shape[1]
    width = wave.shape[2]
    ahead_rows = shifted(wave[0:1], "sector", -1)
    own_full, ahead_full = (
        lax.all_gather(wave, "op", axis=1, tiled=True),
        lax.all_gather(ahead_rows, "op", axis=1, tiled=True),
    )
    following = jnp.concatenate([own_full[1:2], ahead_full], axis=0)
    left_fwd = jnp.einsum("jkac,jcb->jkab", left_ops, own_full, precision=highest)
    left_back = jnp.einsum("jkca,jcb->jkab", left_ops, following, precision=highest)
    weights = coupling.astype(jnp.float32)[:, :, None, None]
    forward = jnp.einsum("jkab,jkcb->jac", weights * left_fwd, right_ops, precision=highest)
    backward = jnp.einsum("jkab,jkbc->jac", weights * left_back, right_ops, precision=highest)
    partial_sums = jnp.stack([backward[0], backward[1] + forward[0]], axis=0)
    leaving = forward[1:2]
    summed, outgoing = (
        lax.psum_scatter(partial_sums, "op", scatter_dimension=1, tiled=True),
        lax.psum_scatter(leaving, "op", scatter_dimension=1, tiled=True),
    )
    arriving = shifted(outgoing, "sector", 1)
    sigma = onsite * wave + summed + jnp.concatenate([arriving, jnp.zeros_like(arriving)], axis=0)
    total = wave.shape[0] * rows * width * lax.axis_size("sector") * lax.axis_size("op")
    norm_sq, energy_sum = lax.psum((jnp.sum(wave * wave), jnp.sum(wave * sigma)), ("sector", "op"))
    energy = energy_sum / norm_sq
    gap = onsite - energy
    first = (sigma - energy * wave) * gap / jnp.maximum(gap * gap, 1.0)
    correlation = lax.psum(jnp.sum(wave * first), ("sector", "op"))
    second = first - correlation / norm_sq * wave
    length_sq = lax.psum(jnp.sum(second * second), ("sector", "op"))
    correction = second * lax.rsqrt(length_sq / total + 1e-06)
    return (sigma, correction)


def solution(mesh):
    return jax.shard_map(
        on_device,
        mesh=mesh,
        in_specs=(
            P("sector", "op", None),
            P("sector", "op", None),
            P("sector", "op", None, None),
            P("sector", "op", None, None),
            P("sector", "op"),
        ),
        out_specs=(P("sector", "op", None), P("sector", "op", None)),
        check_vma=False,
    )
```

profile of v0, /device:TPU:0, one launch (start us, length us, event | category | flops | bytes accessed | tf_op | source)
XLA Modules:
  0.0 506.4 jit_solution(11977234330600486002)
XLA Ops:
  7.2 0.0 all-gather.3.cloned.1.call-start
  7.2 0.7 all-gather.3.cloned.1.call-update
  7.9 0.0 all-gather.5.cloned.1.call-start
  7.9 1.0 slice.19
  8.9 2.5 collective-permute-start
  11.4 4.2 collective-permute-done
  15.6 0.0 copy-start.4
  15.6 0.7 copy-done.4
  16.3 0.0 all-gather.5.cloned.1.call-update
  16.4 0.0 reduce-scatter.5.cloned.1.call-start
  16.4 0.7 convert_element_type.3
  17.1 75.2 %all-gather.3.cloned.1.call-done = f32[2,768,768]{2,1,0:T(8,128)} async-done(((f32[2,96,768]{2,1,0:T(8,128)}), f32[2,768,768]{2,1,0:T(8,128)}) %all-gather.3.cloned.1.call-update) | async-done | bytes 4718608 | tf_op jit(solution)/shard_map/all_gather | solution.py:18
  92.3 0.0 copy-start.1
  92.3 0.0 slice-start.3
  92.3 2.3 copy-done.1
  94.6 0.0 slice-start.4
  94.6 0.0 slice-start.5
  94.6 26.4 %fusion.8 = f32[2,2,768,768]{3,2,1,0:T(8,128)S(1)} fusion(f32[2,2,768,768]{3,2,1,0:T(8,128)} %param.7, f32[2,768,768]{2,1,0:T(8,128)S(1)} %copy-done.1), kind=kOutput, calls=%fused_computation.10 | convolution fusion | flops 21743271936 | bytes 23592960 | tf_op jit(solution)/shard_map/jkac,jcb->jkab/dot_general | solution.py:22
  121.0 0.0 slice-done.3
  121.0 0.0 slice-done.4
  121.0 0.0 slice-done.5
  121.0 0.0 slice-start
  121.0 24.9 %fusion.12 = f32[2,768,768]{2,1,0:T(8,128)} fusion(f32[2,2,768,768]{3,2,1,0:T(8,128)S(1)} %bitcast.28, f32[2,2,768,768]{3,2,1,0:T(8,128)S(1)} %fusion.8, f32[2,2]{1,0:T(2,128)S(1)} %convert_element_type.3), kind=kOutput, calls=%fused_computation.15 | convolution fusion | flops 21745631232 | bytes 23592976 | tf_op jit(solution)/shard_map/jkab,jkcb->jac/dot_general | solution.py:25
  146.0 0.0 slice-done
  146.0 29.8 %fusion.5 = f32[2,768,2,768]{1,3,2,0:T(8,128)S(1)} fusion(f32[2,2,768,768]{3,2,1,0:T(8,128)} %param.7, f32[1,768,768]{2,1,0:T(8,128)} %all-gather.5.cloned.1.call-done, f32[1,768,768]{2,1,0:T(8,128)S(1)} %slice-done), kind=kOutput, calls=%fused_computation.6 | convolution fusion | flops 21744451584 | bytes 23592960 | tf_op jit(solution)/shard_map/jkca,jcb->jkab/dot_general | solution.py:23
  175.8 0.0 slice-start.2
  175.8 25.7 %fusion.15 = f32[2,768,768]{2,1,0:T(8,128)S(1)} fusion(f32[2,2,768,768]{3,2,1,0:T(8,128)} %param.8, f32[2,768,2,768]{1,3,2,0:T(8,128)S(1)} %fusion.5, f32[2,2]{1,0:T(2,128)S(1)} %convert_element_type.3), kind=kOutput, calls=%fused_computation.16 | convolution fusion | flops 21745631232 | bytes 23592976 | tf_op jit(solution)/shard_map/jkab,jkbc->jac/dot_general | solution.py:26
  201.5 0.0 slice-done.1
  201.6 0.0 slice-done.2
  201.6 2.8 fusion.19
  204.3 0.0 reduce-scatter.5.cloned.1.call-update
  204.4 0.0 reduce-scatter.3.cloned.1.call-start
  204.4 4.1 pad_maximum_fusion
  208.5 0.0 reduce-scatter.3.cloned.1.call-update
  208.5 63.8 %reduce-scatter.5.cloned.1.call-done = f32[1,96,768]{2,1,0:T(8,128)} async-done(((f32[1,768,768]{2,1,0:T(8,128)}), f32[1,96,768]{2,1,0:T(8,128)}) %reduce-scatter.5.cloned.1.call-update) | async-done | bytes 294928 | tf_op jit(solution)/shard_map/reduce_scatter | solution.py:31
  272.4 0.0 collective-permute-start.1
  272.4 6.4 %collective-permute-done.1 = f32[1,96,768]{2,1,0:T(8,128)S(1)} collective-permute-done((f32[1,96,768]{2,1,0:T(8,128)}, f32[1,96,768]{2,1,0:T(8,128)S(1)}, u32[]{:S(2)}, u32[]{:S(2)}) %collective-permute-start.1) | collective-permute-done | bytes 294944 | tf_op jit(solution)/shard_map/ppermute | solution.py:9
  278.7 92.0 %reduce-scatter.3.cloned.1.call-done = f32[2,96,768]{2,1,0:T(8,128)} async-done(((f32[2,768,768]{2,1,0:T(8,128)}), f32[2,96,768]{2,1,0:T(8,128)}) %reduce-scatter.3.cloned.1.call-update) | async-done | bytes 589840 | tf_op jit(solution)/shard_map/reduce_scatter | solution.py:30
  370.8 0.0 copy-done
  370.8 0.0 copy-done.2
  370.8 1.8 multiply_reduce_fusion.2
  372.6 40.4 %all-reduce.1 = (f32[]{:T(128)}, f32[]{:T(128)}) all-reduce(f32[]{:T(128)} %get-tuple-element.3, f32[]{:T(128)} %get-tuple-element.2), channel_id=1, replica_groups=mesh['sector'=4,'op'=8] {'sector','op'}, use_global_device_ids=true, to_apply=%region_3.0 | all-reduce | flops 2 | bytes 16 | tf_op jit(solution)/shard_map/psum | solution.py:36
  414.4 0.8 multiply_reduce_fusion.1
  415.2 39.3 %psum.30 = f32[]{:T(128)} all-reduce(f32[]{:T(128)} %multiply_reduce_fusion.1), channel_id=1, replica_groups=mesh['sector'=4,'op'=8] {'sector','op'}, use_global_device_ids=true, to_apply=%region_7.0 | all-reduce | flops 1 | bytes 8 | tf_op jit(solution)/shard_map/psum | solution.py:40
  455.7 0.8 multiply_reduce_fusion
  456.6 41.4 %psum.31 = f32[]{:T(128)} all-reduce(f32[]{:T(128)} %multiply_reduce_fusion), channel_id=1, replica_groups=mesh['sector'=4,'op'=8] {'sector','op'}, use_global_device_ids=true, to_apply=%region_9.0 | all-reduce | flops 1 | bytes 8 | tf_op jit(solution)/shard_map/psum | solution.py:42
  498.6 1.0 broadcast_multiply_fusion
  499.7 0.0 copy-done.3
  (7 shorter events, 0.0 us)
Async XLA Ops:
  7.2 85.1 %all-gather.3.cloned.1.call-start = ((), (), s32[]{:S(2)}) async-start(), calls=%async_computation.2 | async-start | bytes 5308416 | tf_op jit(solution)/shard_map/all_gather | solution.py:18
  7.9 138.1 %all-gather.5.cloned.1.call-start = ((), (), s32[]{:S(2)}) async-start(), calls=%async_computation.3 | async-start | bytes 2654208 | tf_op jit(solution)/shard_map/all_gather | solution.py:19
  8.9 6.7 %collective-permute-start = (f32[1,96,768]{2,1,0:T(8,128)S(1)}, f32[1,96,768]{2,1,0:T(8,128)S(1)}, u32[]{:S(2)}, u32[]{:S(2)}) collective-permute-start(f32[1,96,768]{2,1,0:T(8,128)S(1)} %slice.19), channel_id=1, source_target_pairs={{0,24},{8,0},{16,8},{24,16},{1,25},{9,1},{17,9},{25,17},{2,26},{10... | collective-permute-start | bytes 884744 | tf_op jit(solution)/shard_map/ppermute | solution.py:9
  15.6 0.7 copy-start.4
  16.4 256.0 %reduce-scatter.5.cloned.1.call-start = ((), (), s32[]{:S(2)}) async-start(), calls=%async_computation.5 | async-start | bytes 2654208 | tf_op jit(solution)/shard_map/reduce_scatter | solution.py:31
  92.3 2.3 copy-start.1
  92.3 28.7 %slice-start.3 = ((s8[9437184]{0:T(1024)(128)(4,1)}), s8[4194304]{0:T(1024)(128)(4,1)S(1)}, s32[]{:S(2)}) async-start(s8[9437184]{0:T(1024)(128)(4,1)} %bitcast.27), calls=%async_computation.9 | async-start | bytes 8388608
  94.6 26.4 %slice-start.4 = ((s8[9437184]{0:T(1024)(128)(4,1)}), s8[4194304]{0:T(1024)(128)(4,1)S(1)}, s32[]{:S(2)}) async-start(s8[9437184]{0:T(1024)(128)(4,1)} %bitcast.27), calls=%async_computation.10 | async-start | bytes 8388608
  94.6 26.4 %slice-start.5 = ((s8[9437184]{0:T(1024)(128)(4,1)}), s8[1048576]{0:T(1024)(128)(4,1)S(1)}, s32[]{:S(2)}) async-start(s8[9437184]{0:T(1024)(128)(4,1)} %bitcast.27), calls=%async_computation.11 | async-start | bytes 2097152
  121.0 24.9 %slice-start = ((f32[2,768,768]{2,1,0:T(8,128)}), f32[1,768,768]{2,1,0:T(8,128)S(1)}, s32[]{:S(2)}) async-start(f32[2,768,768]{2,1,0:T(8,128)} %all-gather.3.cloned.1.call-done), calls=%async_computation.6 | async-start | bytes 4718592 | tf_op jit(solution)/shard_map/slice | solution.py:21
  146.0 55.6 %slice-start.1 = ((s8[4718592]{0:T(1024)(128)(4,1)}), s8[4194304]{0:T(1024)(128)(4,1)S(1)}, s32[]{:S(2)}) async-start(s8[4718592]{0:T(1024)(128)(4,1)} %bitcast.25), calls=%async_computation.7 | async-start | bytes 8388608
  175.8 25.7 %slice-start.2 = ((s8[4718592]{0:T(1024)(128)(4,1)}), s8[524288]{0:T(1024)(128)(4,1)S(1)}, s32[]{:S(2)}) async-start(s8[4718592]{0:T(1024)(128)(4,1)} %bitcast.25), calls=%async_computation.8 | async-start | bytes 1048576
  204.4 166.4 %reduce-scatter.3.cloned.1.call-start = ((), (), s32[]{:S(2)}) async-start(), calls=%async_computation.4 | async-start | bytes 5308416 | tf_op jit(solution)/shard_map/reduce_scatter | solution.py:30
  208.5 162.3 %copy-start = (f32[2,96,768]{2,1,0:T(8,128)S(1)}, f32[2,96,768]{2,1,0:T(8,128)}, u32[]{:S(2)}) copy-start(f32[2,96,768]{2,1,0:T(8,128)} %param.5) | copy-start | bytes 1769476
  208.5 162.3 %copy-start.2 = (f32[2,96,768]{2,1,0:T(8,128)S(1)}, f32[2,96,768]{2,1,0:T(8,128)}, u32[]{:S(2)}) copy-start(f32[2,96,768]{2,1,0:T(8,128)} %param.6) | copy-start | bytes 1769476
  272.4 6.4 %collective-permute-start.1 = (f32[1,96,768]{2,1,0:T(8,128)}, f32[1,96,768]{2,1,0:T(8,128)S(1)}, u32[]{:S(2)}, u32[]{:S(2)}) collective-permute-start(f32[1,96,768]{2,1,0:T(8,128)} %reduce-scatter.5.cloned.1.call-done), channel_id=1, source_target_pairs={{0,8},{8,16},{16,24},{24,0},{1,9},{9,17},{17,25},{25,1},{2,10},{10... | collective-permute-start | bytes 884744 | tf_op jit(solution)/shard_map/ppermute | solution.py:9
  372.6 127.0 %copy-start.3 = (f32[2,96,768]{2,1,0:T(8,128)}, f32[2,96,768]{2,1,0:T(8,128)S(1)}, u32[]{:S(2)}) copy-start(f32[2,96,768]{2,1,0:T(8,128)S(1)} %get-tuple-element.6) | copy-start | bytes 1769476
Sparse Core Ops, SparseCore 0:
  10.2 82.0 all-gather.2
  95.0 50.1 all-gather.4
  204.5 67.8 reduce-scatter.4
  275.9 94.8 reduce-scatter.2
where the time goes:
time: 513 us; the launch traced here: 506 us
  waiting for transfers between devices  242 us (47%)
  blocking collectives  121 us (24%)
  matrix products  107 us (21%)
  between operations  17.4 us (3%)
  other arithmetic  12 us (2%)
    reduce_scatter x1, waiting for transfers between devices, on_device(): lax.psum_scatter(partial_sums, 'op', scatter_dimension=1, tiled=True)  92 us
    all_gather x1, waiting for transfers between devices, on_device(): lax.all_gather(wave, 'op', axis=1, tiled=True)  75.2 us
    reduce_scatter x1, waiting for transfers between devices, on_device(): lax.psum_scatter(leaving, 'op', scatter_dimension=1, tiled=True)  63.8 us
    psum x1, blocking collectives, on_device(): length_sq = lax.psum(jnp.sum(second * second), ('sector', 'op'))  41.4 us
    psum x1, blocking collectives, on_device(): lax.psum((jnp.sum(wave * wave), jnp.sum(wave * sigma)), ('sector', 'op'))  40.4 us
    psum x1, blocking collectives, on_device(): correlation = lax.psum(jnp.sum(wave * first), ('sector', 'op'))  39.3 us
    dot_general x1, matrix products, on_device(): jnp.einsum('jkca,jcb->jkab', left_ops, following, precision=highest)  29.8 us
    dot_general x1, matrix products, on_device(): jnp.einsum('jkac,jcb->jkab', left_ops, own_full, precision=highest)  26.4 us
  transfers between devices with their start and end apart: 6, of which 5 were waited for; matrix products, arithmetic and copies ran while one was open for 11% of the time, Pallas kernels for 0%

commit v1 on v0

--- a/solution.py
+++ b/solution.py
@@ -2,6 +2,27 @@
 import jax.numpy as jnp
 from jax import lax
 from jax.sharding import PartitionSpec as P
+
+
+def ring_gather(x, axis, dim):
+    size, index, rows = (lax.axis_size(axis), lax.axis_index(axis), x.shape[dim])
+    right = [(i, (i + 1) % size) for i in range(size)]
+    left = [(i, (i - 1) % size) for i in range(size)]
+    result = jnp.zeros((*x.shape[:dim], size * rows, *x.shape[dim + 1 :]), x.dtype)
+    result = lax.dynamic_update_slice_in_dim(result, x, index * rows, axis=dim)
+    from_left = from_right = x
+    half = size // 2
+    for lap in range(1, half + 1):
+        from_left = lax.ppermute(from_left, axis, right)
+        result = lax.dynamic_update_slice_in_dim(
+            result, from_left, (index - lap) % size * rows, axis=dim
+        )
+        if lap < size - half:
+            from_right = lax.ppermute(from_right, axis, left)
+            result = lax.dynamic_update_slice_in_dim(
+                result, from_right, (index + lap) % size * rows, axis=dim
+            )
+    return result
 
 
 def shifted(value, axis, by):
@@ -15,7 +36,7 @@
     width = wave.shape[2]
     ahead_rows = shifted(wave[0:1], "sector", -1)
     own_full, ahead_full = (
-        lax.all_gather(wave, "op", axis=1, tiled=True),
+        ring_gather(wave, "op", 1),
         lax.all_gather(ahead_rows, "op", axis=1, tiled=True),
     )
     following = jnp.concatenate([own_full[1:2], ahead_full], axis=0)

time: 513 us -> 539 us (1.051)
  waiting for transfers between devices: 242 us -> 260 us
  starting transfers between devices: 2.62 us -> 13.8 us
    ppermute x0 -> x7, waiting for transfers between devices: none -> 97.2 us  [the longest x4 66.9 us: ring_gather(): from_left = lax.ppermute(from_left, axis, right)]
    all_gather x1 -> x0, waiting for transfers between devices: 75.2 us -> none  [on_device(): lax.all_gather(wave, 'op', axis=1, tiled=True)]
    ppermute x0 -> x7, starting transfers between devices: none -> 13 us  [the longest x4 7.91 us: ring_gather(): from_left = lax.ppermute(from_left, axis, right)]
  transfers between devices with their start and end apart: 6 -> 12, of which waited for: 5 -> 10; matrix products, arithmetic and copies ran while one was open for 11% -> 11% of each run, Pallas kernels for 0% -> 0%
where the time goes in v1:
time: 539 us; the launch traced here: 533 us
  waiting for transfers between devices  260 us (48%)
  blocking collectives  121 us (22%)
  matrix products  106 us (20%)
  between operations  17.6 us (3%)
  starting transfers between devices  13.8 us (3%)
  other arithmetic  12.2 us (2%)
    reduce_scatter x1, waiting for transfers between devices, on_device(): lax.psum_scatter(partial_sums, 'op', scatter_dimension=1, tiled=True)  92.2 us
    ppermute x4, waiting for transfers between devices, ring_gather(): from_left = lax.ppermute(from_left, axis, right)  66.9 us
    reduce_scatter x1, waiting for transfers between devices, on_device(): lax.psum_scatter(leaving, 'op', scatter_dimension=1, tiled=True)  63.1 us
    psum x1, blocking collectives, on_device(): length_sq = lax.psum(jnp.sum(second * second), ('sector', 'op'))  41.4 us
    psum x1, blocking collectives, on_device(): lax.psum((jnp.sum(wave * wave), jnp.sum(wave * sigma)), ('sector', 'op'))  40.4 us
    psum x1, blocking collectives, on_device(): correlation = lax.psum(jnp.sum(wave * first), ('sector', 'op'))  39.3 us
    ppermute x3, waiting for transfers between devices, ring_gather(): from_right = lax.ppermute(from_right, axis, left)  30.3 us
    dot_general x1, matrix products, on_device(): jnp.einsum('jkca,jcb->jkab', left_ops, following, precision=highest)  29.8 us
  transfers between devices with their start and end apart: 12, of which 10 were waited for; matrix products, arithmetic and copies ran while one was open for 11% of the time, Pallas kernels for 0%

profile of v1, /device:TPU:0, one launch (start us, length us, event | category | flops | bytes accessed | tf_op | source)
XLA Modules:
  0.0 532.7 jit_solution(12677223844096899724)
XLA Ops:
  7.2 0.0 copy-start.1
  7.2 0.0 all-gather.2.cloned.1.call-start
  7.2 3.0 collective-permute-start
  10.3 1.0 slice.19
  11.3 0.7 collective-permute-start.7
  12.0 3.4 collective-permute-start.1
  15.4 0.9 collective-permute-done.7
  16.2 0.7 copy-done.4
  16.9 0.0 all-gather.2.cloned.1.call-update
  17.0 0.0 reduce-scatter.5.cloned.1.call-start
  17.0 22.0 %collective-permute-done = f32[2,96,768]{2,1,0:T(8,128)S(1)} collective-permute-done((f32[2,96,768]{2,1,0:T(8,128)}, f32[2,96,768]{2,1,0:T(8,128)S(1)}, u32[]{:S(2)}, u32[]{:S(2)}) %collective-permute-start) | collective-permute-done | bytes 589856 | tf_op jit(solution)/shard_map/ppermute | solution.py:16
  39.0 2.4 collective-permute-start.2
  41.3 1.3 collective-permute-done.1
  42.6 1.7 collective-permute-start.3
  44.4 34.0 %collective-permute-done.2 = f32[2,96,768]{2,1,0:T(8,128)S(1)} collective-permute-done((f32[2,96,768]{2,1,0:T(8,128)S(1)}, f32[2,96,768]{2,1,0:T(8,128)S(1)}, u32[]{:S(2)}, u32[]{:S(2)}) %collective-permute-start.2) | collective-permute-done | bytes 589856 | tf_op jit(solution)/shard_map/ppermute | solution.py:16
  78.4 2.5 collective-permute-start.4
  80.9 0.7 convert_element_type.3
  81.6 0.3 broadcast_in_dim.2
  81.9 8.8 %collective-permute-done.3 = f32[2,96,768]{2,1,0:T(8,128)S(1)} collective-permute-done((f32[2,96,768]{2,1,0:T(8,128)S(1)}, f32[2,96,768]{2,1,0:T(8,128)S(1)}, u32[]{:S(2)}, u32[]{:S(2)}) %collective-permute-start.3) | collective-permute-done | bytes 589856 | tf_op jit(solution)/shard_map/ppermute | solution.py:21
  90.8 0.0 collective-permute-start.5
  90.8 10.9 %collective-permute-done.4 = f32[2,96,768]{2,1,0:T(8,128)S(1)} collective-permute-done((f32[2,96,768]{2,1,0:T(8,128)S(1)}, f32[2,96,768]{2,1,0:T(8,128)S(1)}, u32[]{:S(2)}, u32[]{:S(2)}) %collective-permute-start.4) | collective-permute-done | bytes 589856 | tf_op jit(solution)/shard_map/ppermute | solution.py:16
  101.8 0.0 collective-permute-start.6
  101.9 0.0 copy-start
  102.0 20.2 %collective-permute-done.5 = f32[2,96,768]{2,1,0:T(8,128)S(1)} collective-permute-done((f32[2,96,768]{2,1,0:T(8,128)S(1)}, f32[2,96,768]{2,1,0:T(8,128)S(1)}, u32[]{:S(2)}, u32[]{:S(2)}) %collective-permute-start.5) | collective-permute-done | bytes 589856 | tf_op jit(solution)/shard_map/ppermute | solution.py:21
  122.2 0.0 collective-permute-done.6
  122.3 0.0 slice-start.2
  122.3 0.2 slice.24
  122.5 0.0 slice-start.3
  122.5 0.0 slice-start.4
  122.5 25.2 %fusion.9 = f32[2,768,2,768]{1,3,2,0:T(8,128)S(1)} fusion(f32[2,2,768,768]{3,2,1,0:T(8,128)S(1)} %copy-done, f32[2,768,768]{2,1,0:T(8,128)S(1)} %constant_dynamic-update-slice_fusion), kind=kOutput, calls=%fused_computation.11 | convolution fusion | flops 21743271936 | bytes 23592960 | tf_op jit(solution)/shard_map/jkac,jcb->jkab/dot_general | solution.py:43
  147.7 24.9 %fusion.16 = f32[2,768,768]{2,1,0:T(8,128)} fusion(f32[2,2,768,768]{3,2,1,0:T(8,128)S(1)} %bitcast.33, f32[2,768,2,768]{1,3,2,0:T(8,128)S(1)} %fusion.9, f32[2,2]{1,0:T(2,128)S(1)} %convert_element_type.3), kind=kOutput, calls=%fused_computation.17 | convolution fusion | flops 21745631232 | bytes 23592976 | tf_op jit(solution)/shard_map/jkab,jkcb->jac/dot_general | solution.py:46
  172.6 29.8 %fusion.6 = f32[2,768,2,768]{1,3,2,0:T(8,128)S(1)} fusion(f32[2,2,768,768]{3,2,1,0:T(8,128)} %param.7, f32[1,768,768]{2,1,0:T(8,128)} %all-gather.2.cloned.1.call-done, f32[1,768,768]{2,1,0:T(8,128)S(1)} %slice.24), kind=kOutput, calls=%fused_computation.7 | convolution fusion | flops 21744451584 | bytes 23592960 | tf_op jit(solution)/shard_map/jkca,jcb->jkab/dot_general | solution.py:44
  202.4 25.7 %fusion.13 = f32[2,768,768]{2,1,0:T(8,128)S(1)} fusion(f32[2,2,768,768]{3,2,1,0:T(8,128)} %param.8, f32[2,768,2,768]{1,3,2,0:T(8,128)S(1)} %fusion.6, f32[2,2]{1,0:T(2,128)S(1)} %convert_element_type.3), kind=kOutput, calls=%fused_computation.16 | convolution fusion | flops 21745631232 | bytes 23592976 | tf_op jit(solution)/shard_map/jkab,jkbc->jac/dot_general | solution.py:47
  228.2 2.8 fusion.20
  230.9 0.0 reduce-scatter.5.cloned.1.call-update
  231.0 0.0 reduce-scatter.3.cloned.1.call-start
  231.0 4.1 pad_maximum_fusion
  235.1 0.0 reduce-scatter.3.cloned.1.call-update
  235.1 63.1 %reduce-scatter.5.cloned.1.call-done = f32[1,96,768]{2,1,0:T(8,128)} async-done(((f32[1,768,768]{2,1,0:T(8,128)}), f32[1,96,768]{2,1,0:T(8,128)}) %reduce-scatter.5.cloned.1.call-update) | async-done | bytes 294928 | tf_op jit(solution)/shard_map/reduce_scatter | solution.py:52
  298.3 6.4 %collective-permute-done.8 = f32[1,96,768]{2,1,0:T(8,128)S(1)} collective-permute-done((f32[1,96,768]{2,1,0:T(8,128)}, f32[1,96,768]{2,1,0:T(8,128)S(1)}, u32[]{:S(2)}, u32[]{:S(2)}) %collective-permute-start.8) | collective-permute-done | bytes 294944 | tf_op jit(solution)/shard_map/ppermute | solution.py:30
  304.6 92.2 %reduce-scatter.3.cloned.1.call-done = f32[2,96,768]{2,1,0:T(8,128)} async-done(((f32[2,768,768]{2,1,0:T(8,128)}), f32[2,96,768]{2,1,0:T(8,128)}) %reduce-scatter.3.cloned.1.call-update) | async-done | bytes 589840 | tf_op jit(solution)/shard_map/reduce_scatter | solution.py:51
  396.9 1.9 multiply_reduce_fusion.2
  398.8 40.4 %all-reduce.1 = (f32[]{:T(128)}, f32[]{:T(128)}) all-reduce(f32[]{:T(128)} %get-tuple-element.3, f32[]{:T(128)} %get-tuple-element.2), channel_id=1, replica_groups=mesh['sector'=4,'op'=8] {'sector','op'}, use_global_device_ids=true, to_apply=%region_3.4 | all-reduce | flops 2 | bytes 16 | tf_op jit(solution)/shard_map/psum | solution.py:57
  440.5 0.8 multiply_reduce_fusion.1
  441.4 39.3 %psum.30 = f32[]{:T(128)} all-reduce(f32[]{:T(128)} %multiply_reduce_fusion.1), channel_id=1, replica_groups=mesh['sector'=4,'op'=8] {'sector','op'}, use_global_device_ids=true, to_apply=%region_7.8 | all-reduce | flops 1 | bytes 8 | tf_op jit(solution)/shard_map/psum | solution.py:61
  482.0 0.8 multiply_reduce_fusion
  482.8 41.4 %psum.31 = f32[]{:T(128)} all-reduce(f32[]{:T(128)} %multiply_reduce_fusion), channel_id=1, replica_groups=mesh['sector'=4,'op'=8] {'sector','op'}, use_global_device_ids=true, to_apply=%region_9.10 | all-reduce | flops 1 | bytes 8 | tf_op jit(solution)/shard_map/psum | solution.py:63
  524.9 1.0 broadcast_multiply_fusion
  (26 shorter events, 0.4 us)
Async XLA Ops:
  7.2 74.7 %copy-start.1 = (f32[2,96,768]{2,1,0:T(8,128)S(1)}, f32[2,96,768]{2,1,0:T(8,128)}, u32[]{:S(2)}) copy-start(f32[2,96,768]{2,1,0:T(8,128)} %param.5) | copy-start | bytes 1769476
  7.2 165.4 %all-gather.2.cloned.1.call-start = ((), (), s32[]{:S(2)}) async-start(), calls=%async_computation.2 | async-start | bytes 2654208 | tf_op jit(solution)/shard_map/all_gather | solution.py:40
  7.2 31.8 %collective-permute-start = (f32[2,96,768]{2,1,0:T(8,128)}, f32[2,96,768]{2,1,0:T(8,128)S(1)}, u32[]{:S(2)}, u32[]{:S(2)}) collective-permute-start(f32[2,96,768]{2,1,0:T(8,128)} %param.5), channel_id=1, source_target_pairs={{0,1},{1,2},{2,3},{3,4},{4,5},{5,6},{6,7},{7,0},{8,9},{9,10},{10,1... | collective-permute-start | bytes 1769480 | tf_op jit(solution)/shard_map/ppermute | solution.py:16
  11.3 4.9 collective-permute-start.7
  12.0 30.7 %collective-permute-start.1 = (f32[2,96,768]{2,1,0:T(8,128)}, f32[2,96,768]{2,1,0:T(8,128)S(1)}, u32[]{:S(2)}, u32[]{:S(2)}) collective-permute-start(f32[2,96,768]{2,1,0:T(8,128)} %param.5), channel_id=1, source_target_pairs={{0,7},{1,0},{2,1},{3,2},{4,3},{5,4},{6,5},{7,6},{8,15},{9,8},{10,9... | collective-permute-start | bytes 1769480 | tf_op jit(solution)/shard_map/ppermute | solution.py:21
  16.2 0.7 copy-start.4
  17.0 281.3 %reduce-scatter.5.cloned.1.call-start = ((), (), s32[]{:S(2)}) async-start(), calls=%async_computation.4 | async-start | bytes 2654208 | tf_op jit(solution)/shard_map/reduce_scatter | solution.py:52
  39.0 39.4 %collective-permute-start.2 = (f32[2,96,768]{2,1,0:T(8,128)S(1)}, f32[2,96,768]{2,1,0:T(8,128)S(1)}, u32[]{:S(2)}, u32[]{:S(2)}) collective-permute-start(f32[2,96,768]{2,1,0:T(8,128)S(1)} %collective-permute-done), channel_id=1, source_target_pairs={{0,1},{1,2},{2,3},{3,4},{4,5},{5,6},{6,7},{7,0},{8,9},{9,10},{10,1... | collective-permute-start | bytes 1769480 | tf_op jit(solution)/shard_map/ppermute | solution.py:16
  42.6 48.1 %collective-permute-start.3 = (f32[2,96,768]{2,1,0:T(8,128)S(1)}, f32[2,96,768]{2,1,0:T(8,128)S(1)}, u32[]{:S(2)}, u32[]{:S(2)}) collective-permute-start(f32[2,96,768]{2,1,0:T(8,128)S(1)} %collective-permute-done.1), channel_id=1, source_target_pairs={{0,7},{1,0},{2,1},{3,2},{4,3},{5,4},{6,5},{7,6},{8,15},{9,8},{10,9... | collective-permute-start | bytes 1769480 | tf_op jit(solution)/shard_map/ppermute | solution.py:21
  78.4 23.4 %collective-permute-start.4 = (f32[2,96,768]{2,1,0:T(8,128)S(1)}, f32[2,96,768]{2,1,0:T(8,128)S(1)}, u32[]{:S(2)}, u32[]{:S(2)}) collective-permute-start(f32[2,96,768]{2,1,0:T(8,128)S(1)} %collective-permute-done.2), channel_id=1, source_target_pairs={{0,1},{1,2},{2,3},{3,4},{4,5},{5,6},{6,7},{7,0},{8,9},{9,10},{10,1... | collective-permute-start | bytes 1769480 | tf_op jit(solution)/shard_map/ppermute | solution.py:16
  90.8 31.4 %collective-permute-start.5 = (f32[2,96,768]{2,1,0:T(8,128)S(1)}, f32[2,96,768]{2,1,0:T(8,128)S(1)}, u32[]{:S(2)}, u32[]{:S(2)}) collective-permute-start(f32[2,96,768]{2,1,0:T(8,128)S(1)} %collective-permute-done.3), channel_id=1, source_target_pairs={{0,7},{1,0},{2,1},{3,2},{4,3},{5,4},{6,5},{7,6},{8,15},{9,8},{10,9... | collective-permute-start | bytes 1769480 | tf_op jit(solution)/shard_map/ppermute | solution.py:21
  101.8 20.4 %collective-permute-start.6 = (f32[2,96,768]{2,1,0:T(8,128)S(1)}, f32[2,96,768]{2,1,0:T(8,128)S(1)}, u32[]{:S(2)}, u32[]{:S(2)}) collective-permute-start(f32[2,96,768]{2,1,0:T(8,128)S(1)} %collective-permute-done.4), channel_id=1, source_target_pairs={{0,1},{1,2},{2,3},{3,4},{4,5},{5,6},{6,7},{7,0},{8,9},{9,10},{10,1... | collective-permute-start | bytes 1769480 | tf_op jit(solution)/shard_map/ppermute | solution.py:16
  101.9 20.6 %copy-start = (f32[2,2,768,768]{3,2,1,0:T(8,128)S(1)}, f32[2,2,768,768]{3,2,1,0:T(8,128)}, u32[]{:S(2)}) copy-start(f32[2,2,768,768]{3,2,1,0:T(8,128)} %param.7) | copy-start | bytes 28311556
  122.3 25.4 %slice-start.2 = ((s8[9437184]{0:T(1024)(128)(4,1)}), s8[4194304]{0:T(1024)(128)(4,1)S(1)}, s32[]{:S(2)}) async-start(s8[9437184]{0:T(1024)(128)(4,1)} %bitcast.32), calls=%async_computation.7 | async-start | bytes 8388608
  122.5 25.2 %slice-start.3 = ((s8[9437184]{0:T(1024)(128)(4,1)}), s8[4194304]{0:T(1024)(128)(4,1)S(1)}, s32[]{:S(2)}) async-start(s8[9437184]{0:T(1024)(128)(4,1)} %bitcast.32), calls=%async_computation.8 | async-start | bytes 8388608
  122.5 25.2 %slice-start.4 = ((s8[9437184]{0:T(1024)(128)(4,1)}), s8[1048576]{0:T(1024)(128)(4,1)S(1)}, s32[]{:S(2)}) async-start(s8[9437184]{0:T(1024)(128)(4,1)} %bitcast.32), calls=%async_computation.9 | async-start | bytes 2097152
  172.6 55.5 %slice-start = ((s8[4718592]{0:T(1024)(128)(4,1)}), s8[4194304]{0:T(1024)(128)(4,1)S(1)}, s32[]{:S(2)}) async-start(s8[4718592]{0:T(1024)(128)(4,1)} %bitcast.30), calls=%async_computation.5 | async-start | bytes 8388608
  202.4 25.7 %slice-start.1 = ((s8[4718592]{0:T(1024)(128)(4,1)}), s8[524288]{0:T(1024)(128)(4,1)S(1)}, s32[]{:S(2)}) async-start(s8[4718592]{0:T(1024)(128)(4,1)} %bitcast.30), calls=%async_computation.6 | async-start | bytes 1048576
  231.0 165.9 %reduce-scatter.3.cloned.1.call-start = ((), (), s32[]{:S(2)}) async-start(), calls=%async_computation.3 | async-start | bytes 5308416 | tf_op jit(solution)/shard_map/reduce_scatter | solution.py:51
  235.1 161.8 %copy-start.2 = (f32[2,96,768]{2,1,0:T(8,128)S(1)}, f32[2,96,768]{2,1,0:T(8,128)}, u32[]{:S(2)}) copy-start(f32[2,96,768]{2,1,0:T(8,128)} %param.6) | copy-start | bytes 1769476
  298.3 6.4 %collective-permute-start.8 = (f32[1,96,768]{2,1,0:T(8,128)}, f32[1,96,768]{2,1,0:T(8,128)S(1)}, u32[]{:S(2)}, u32[]{:S(2)}) collective-permute-start(f32[1,96,768]{2,1,0:T(8,128)} %reduce-scatter.5.cloned.1.call-done), channel_id=1, source_target_pairs={{0,8},{8,16},{16,24},{24,0},{1,9},{9,17},{17,25},{25,1},{2,10},{10... | collective-permute-start | bytes 884744 | tf_op jit(solution)/shard_map/ppermute | solution.py:30
  398.8 127.2 %copy-start.3 = (f32[2,96,768]{2,1,0:T(8,128)}, f32[2,96,768]{2,1,0:T(8,128)S(1)}, u32[]{:S(2)}) copy-start(f32[2,96,768]{2,1,0:T(8,128)S(1)} %get-tuple-element.6) | copy-start | bytes 1769476
Sparse Core Ops, SparseCore 0:
  17.1 87.5 all-gather.1
  231.1 67.1 reduce-scatter.4
  301.9 94.9 reduce-scatter.2
